TPU v7x, 32 devices: a whole 2x2x4 slice. The times are simulated.
32 devices in a mesh: replica: 4 (over y, x), fsdp: 8 (over z, core).
Axes of the slice: x: 2, y: 2, z: 4, core: 2. Of those that a mesh axis runs over, the one named last changes fastest.
Arguments:
- local_weights: bfloat16 [4, 256, 28672], P('replica', 'fsdp'), may hold values from -6 to 6
- base_weights: float32 [256, 28672], P('fsdp'), may hold values from -6 to 6
- momentum: float32 [256, 28672], P('replica', 'fsdp'), may hold values from -4 to 4
Outputs:
- new_weights: float32 [256, 28672], P('fsdp')
- new_momentum: float32 [256, 28672], P('replica', 'fsdp')
All inputs are finite; a program needn't handle non-finite values. Where the computation divides by a largest or mean magnitude, that divisor is 1e-20 or more.
Results may differ from a plain program's by a relative error of at most 0.015.
Values may be sent and summed in bfloat16 or wider, within the bound.
A program may use at most 128 MiB of HBM per device.

v0:
```python
import jax
import jax.numpy as jnp
from jax import lax
from jax.sharding import PartitionSpec as P

QBLOCK = 128


EPSILON = 1e-06
LEARN_RATE = 0.7
MOMENTUM_COEF = 0.9


def dequantise(integer_levels, block_scales):
    shaped = integer_levels.astype(jnp.float32).reshape(block_scales.shape + (QBLOCK,))
    values = shaped * block_scales.astype(jnp.float32)[..., None]
    return values.reshape(integer_levels.shape)


def per_device(local_weights, base_weights, momentum):
    row_count, col_count = base_weights.shape
    replica_differences = base_weights - local_weights[0].astype(jnp.float32)
    block_grouped = replica_differences.reshape(row_count, col_count // QBLOCK, QBLOCK)
    block_scales = (jnp.max(jnp.abs(block_grouped), axis=2) + EPSILON).astype(jnp.bfloat16)
    integer_levels = (block_grouped / block_scales.astype(jnp.float32)[:, :, None]).astype(
        jnp.bfloat16
    )
    levels_local = integer_levels.reshape(1, row_count, col_count)
    scales_local = block_scales.reshape(1, row_count, col_count // QBLOCK)
    replica_count = lax.axis_size("replica")
    shard_group_count = lax.axis_size("fsdp")
    group = shard_group_count // replica_count
    piece = momentum.shape[1] // shard_group_count
    levels_owned, scales_owned = (
        lax.all_to_all(levels_local, "replica", split_axis=2, concat_axis=0, tiled=True),
        lax.all_to_all(scales_local, "replica", split_axis=2, concat_axis=0, tiled=True),
    )
    summed = jnp.sum(dequantise(levels_owned, scales_owned), axis=0)
    sectioned = momentum.reshape(group, row_count, shard_group_count, piece)
    sectioned = lax.all_to_all(sectioned, "fsdp", split_axis=2, concat_axis=2, tiled=True)
    sectioned = lax.all_to_all(sectioned, "replica", split_axis=2, concat_axis=0, tiled=True)
    sectioned = lax.all_to_all(sectioned, "fsdp", split_axis=0, concat_axis=3, tiled=True)
    owned_momentum = sectioned.reshape(row_count, col_count // replica_count)
    average = summed / replica_count
    owned_new = MOMENTUM_COEF * owned_momentum + average
    update = (LEARN_RATE * (average + MOMENTUM_COEF * owned_new)).astype(jnp.bfloat16)
    returned = lax.all_gather(update, "replica", axis=1, tiled=True)
    going = owned_new.reshape(1, row_count, group, shard_group_count * piece)
    going = lax.all_to_all(going, "fsdp", split_axis=3, concat_axis=0, tiled=True)
    going = lax.all_to_all(going, "replica", split_axis=0, concat_axis=2, tiled=True)
    going = lax.all_to_all(going, "fsdp", split_axis=2, concat_axis=2, tiled=True)
    new_momentum = going.reshape(momentum.shape)
    new_weights = base_weights - returned.astype(jnp.float32)
    return (new_weights, new_momentum)


def solution(mesh):
    return jax.shard_map(
        per_device,
        mesh=mesh,
        in_specs=(P("replica", "fsdp", None), P("fsdp", None), P("replica", "fsdp")),
        out_specs=(P("fsdp", None), P("replica", "fsdp")),
        check_vma=False,
    )
```

profile of v0, /device:TPU:7, one launch (start us, length us, event | category | flops | bytes accessed | tf_op | source)
XLA Modules:
  0.0 442.0 jit_solution(15897536443774673228)
XLA Ops:
  7.2 3.0 abs_bitcast_fusion
  10.2 2.5 copy.72
  12.6 3.3 reduce_max.9
  16.1 0.5 broadcast.56
  16.6 1.0 reduce.3
  17.6 0.7 reshape.110
  18.3 3.6 all-to-all-start.1
  21.9 1.0 div.20
  23.0 1.0 copy-done
  24.0 3.6 fusion.2
  27.6 27.0 %copy.56 = bf16[1,32,28672]{1,0,2:T(2,128)(2,1)} copy(bf16[1,32,28672]{2,1,0:T(8,128)(2,1)} %fusion.2) | data formatting | bytes 3670016 | tf_op jit(solution)/shard_map/convert_element_type | solution.py:25
  54.6 157.0 %reduce.2 = bf16[28672,32]{1,0:T(8,128)(2,1)} reduce(bf16[28672,1,32]{2,1,0:T(2,128)(2,1)} %bitcast.64, bf16[]{:T(256)} %broadcast.56), dimensions={1}, to_apply=%bitcast.56.reduce_sub_computation | reduce | bytes 3670018
  211.6 9.4 %reshape.108 = bf16[4,2,114688]{2,1,0:T(2,128)(2,1)} reshape(bf16[28672,32]{1,0:T(8,128)(2,1)} %reduce.2) | data formatting | bytes 3670016
  221.0 3.9 all-to-all-start
  225.0 1.5 reshape.102
  226.4 1.8 copy.59
  228.3 16.3 %all-to-all-done = bf16[4,2,114688]{2,1,0:T(2,128)(2,1)S(1)} async-done(((bf16[4,2,114688]{2,1,0:T(2,128)(2,1)}), bf16[4,2,114688]{2,1,0:T(2,128)(2,1)S(1)}, u32[]{:S(2)}, u32[]{:S(2)}) %all-to-all-start) | async-done | bytes 1835040 | tf_op jit(solution)/shard_map/all_to_all | solution.py:35
  244.5 32.5 %all_to_all.91 = f32[2,32,8,448]{3,1,0,2:T(8,128)} all-to-all(f32[2,32,8,448]{3,1,0,2:T(8,128)S(1)} %copy.59), channel_id=1, replica_groups=mesh['replica'=4,'fsdp'=8] {'fsdp'}, dimensions={2} | all-to-all | bytes 1835008 | tf_op jit(solution)/shard_map/all_to_all | solution.py:40
  277.0 4.7 %all-to-all-start.3 = ((f32[2,32,8,448]{3,1,0,2:T(8,128)}), f32[2,32,8,448]{3,1,0,2:T(8,128)S(1)}, u32[]{:S(2)}, u32[]{:S(2)}) async-start(f32[2,32,8,448]{3,1,0,2:T(8,128)} %all_to_all.91), calls=%async_computation.3 | async-start | bytes 2097152 | tf_op jit(solution)/shard_map/all_to_all | solution.py:41
  282.0 8.1 %reshape.109 = bf16[28672,1,32]{2,1,0:T(2,128)(2,1)} reshape(bf16[4,2,114688]{2,1,0:T(2,128)(2,1)S(1)} %all-to-all-done) | data formatting | bytes 3670016
  290.1 3.1 all-to-all-done.3
  293.2 1.8 copy.60
  295.1 5.3 %all-to-all-start.4 = ((f32[8,32,2,448]{3,2,1,0:T(2,128)}), f32[8,32,2,448]{3,2,1,0:T(2,128)S(1)}, u32[]{:S(2)}, u32[]{:S(2)}) async-start(f32[8,32,2,448]{3,2,1,0:T(2,128)} %bitcast.71), calls=%async_computation.4 | async-start | bytes 2097152 | tf_op jit(solution)/shard_map/all_to_all | solution.py:42
  300.4 17.6 %bitcast_convert_fusion = f32[1,32,28672]{1,0,2:T(1,128)} fusion(bf16[28672,1,32]{2,1,0:T(2,128)(2,1)} %reshape.109), kind=kLoop, calls=%fused_computation.15 | loop fusion | flops 917504 | bytes 5505024 | tf_op jit(solution)/shard_map/convert_element_type | solution.py:15
  318.0 8.9 %fusion = f32[32,7168]{0,1:T(8,128)} fusion(f32[4,1,32,7168]{2,3,0,1:T(8,128)} %bitcast.65, f32[4,32,56]{1,2,0:T(8,128)S(1)} %bitcast.76), kind=kLoop, calls=%fused_computation.1 | loop fusion | flops 1605632 | bytes 4616192 | tf_op jit(solution)/shard_map/reduce_sum | solution.py:38
  326.9 3.3 copy.58
  330.2 0.5 multiply_bitcast_fusion
  330.7 0.6 copy.61
  331.3 0.6 copy.62
  332.0 0.4 mul.52
  332.4 2.2 broadcast_multiply_fusion
  334.5 0.8 div.25
  335.3 0.4 mul.56
  335.8 0.2 copy_add_fusion
  336.0 3.6 copy.64
  339.6 5.2 %reshape.112 = f32[8,1,28672]{2,1,0:T(1,128)S(1)} reshape(f32[3584,1,2,32]{3,2,1,0:T(2,128)} %bitcast.67) | data formatting | bytes 1835008
  344.8 27.8 %all_to_all.92 = f32[8,1,28672]{2,1,0:T(1,128)S(1)} all-to-all(f32[8,1,28672]{2,1,0:T(1,128)S(1)} %reshape.112), channel_id=1, replica_groups=mesh['replica'=4,'fsdp'=8] {'fsdp'}, dimensions={0} | all-to-all | bytes 1835008 | tf_op jit(solution)/shard_map/all_to_all | solution.py:49
  372.6 0.5 broadcast.58
  373.1 2.8 reduce.4
  375.9 4.9 %reshape.113 = f32[3584,1,2,32]{3,2,1,0:T(2,128)} reshape(f32[8,28672]{1,0:T(8,128)S(1)} %reduce.4) | data formatting | bytes 1835008
  380.9 5.0 %copy.71 = f32[1,32,2,8,448]{4,1,2,3,0:T(8,128)S(1)} copy(f32[1,32,2,8,448]{1,2,4,3,0:T(2,128)} %bitcast.68) | data formatting | bytes 1835008 | tf_op jit(solution)/shard_map/all_to_all | solution.py:49
  385.9 15.1 %all_to_all.93 = f32[8,32,2,448]{3,1,2,0:T(8,128)S(1)} all-to-all(f32[8,32,2,448]{3,1,2,0:T(8,128)S(1)} %bitcast.74), channel_id=1, replica_groups=mesh['replica'=4,'fsdp'=8] {'replica'}, dimensions={0} | all-to-all | bytes 1835008 | tf_op jit(solution)/shard_map/all_to_all | solution.py:50
  401.1 1.1 copy.68
  402.2 5.4 %all-to-all-start.7 = ((f32[2,32,8,448]{3,1,0,2:T(8,128)}), f32[2,32,8,448]{3,1,0,2:T(8,128)S(1)}, u32[]{:S(2)}, u32[]{:S(2)}) async-start(f32[2,32,8,448]{3,1,0,2:T(8,128)} %copy.68), calls=%async_computation.7 | async-start | bytes 2097152 | tf_op jit(solution)/shard_map/all_to_all | solution.py:51
  407.6 4.7 %convert_subtract_fusion.1 = f32[32,28672]{1,0:T(8,128)} fusion(f32[32,28672]{1,0:T(8,128)} %param.4, bf16[32,28672]{1,0:T(8,128)(2,1)} %all-gather.2.cloned.1.call-done), kind=kLoop, calls=%fused_computation.5 | loop fusion | flops 1835008 | bytes 9175040 | tf_op jit(solution)/shard_map/sub | solution.py:53
  412.3 20.9 %all-to-all-done.7 = f32[2,32,8,448]{3,1,0,2:T(8,128)S(1)} async-done(((f32[2,32,8,448]{3,1,0,2:T(8,128)}), f32[2,32,8,448]{3,1,0,2:T(8,128)S(1)}, u32[]{:S(2)}, u32[]{:S(2)}) %all-to-all-start.7) | async-done | bytes 917536 | tf_op jit(solution)/shard_map/all_to_all | solution.py:51
  433.2 0.6 copy.69
  433.8 1.3 reshape.103
  (15 shorter events, 0.5 us)
Async XLA Ops:
  12.6 10.3 %copy-start.1 = (bf16[1,32,28672]{2,1,0:T(8,128)(2,1)S(1)}, bf16[1,32,28672]{2,1,0:T(8,128)(2,1)}, u32[]{:S(2)}) copy-start(bf16[1,32,28672]{2,1,0:T(8,128)(2,1)} %param.3) | copy-start | bytes 5505028
  18.3 202.7 %all-to-all-start.1 = ((bf16[4,2,896]{2,1,0:T(2,128)(2,1)}), bf16[4,2,896]{2,1,0:T(2,128)(2,1)S(1)}, u32[]{:S(2)}, u32[]{:S(2)}) async-start(bf16[4,2,896]{2,1,0:T(2,128)(2,1)} %reshape.110), calls=%async_computation.1 | async-start | bytes 28672 | tf_op jit(solution)/shard_map/all_to_all | solution.py:36
  21.9 2.0 copy-start
  221.0 3.9 copy-start.2
  221.0 23.5 %all-to-all-start = ((bf16[4,2,114688]{2,1,0:T(2,128)(2,1)}), bf16[4,2,114688]{2,1,0:T(2,128)(2,1)S(1)}, u32[]{:S(2)}, u32[]{:S(2)}) async-start(bf16[4,2,114688]{2,1,0:T(2,128)(2,1)} %reshape.108), calls=%async_computation | async-start | bytes 3670016 | tf_op jit(solution)/shard_map/all_to_all | solution.py:35
  277.0 16.2 %all-to-all-start.3 = ((f32[2,32,8,448]{3,1,0,2:T(8,128)}), f32[2,32,8,448]{3,1,0,2:T(8,128)S(1)}, u32[]{:S(2)}, u32[]{:S(2)}) async-start(f32[2,32,8,448]{3,1,0,2:T(8,128)} %all_to_all.91), calls=%async_computation.3 | async-start | bytes 2097152 | tf_op jit(solution)/shard_map/all_to_all | solution.py:41
  295.1 35.1 %all-to-all-start.4 = ((f32[8,32,2,448]{3,2,1,0:T(2,128)}), f32[8,32,2,448]{3,2,1,0:T(2,128)S(1)}, u32[]{:S(2)}, u32[]{:S(2)}) async-start(f32[8,32,2,448]{3,2,1,0:T(2,128)} %bitcast.71), calls=%async_computation.4 | async-start | bytes 2097152 | tf_op jit(solution)/shard_map/all_to_all | solution.py:42
  300.4 107.2 %all-gather.2.cloned.1.call-start = ((), (), s32[]{:S(2)}) async-start(), calls=%async_computation.8 | async-start | bytes 2293760 | tf_op jit(solution)/shard_map/all_gather | solution.py:47
  402.2 31.0 %all-to-all-start.7 = ((f32[2,32,8,448]{3,1,0,2:T(8,128)}), f32[2,32,8,448]{3,1,0,2:T(8,128)S(1)}, u32[]{:S(2)}, u32[]{:S(2)}) async-start(f32[2,32,8,448]{3,1,0,2:T(8,128)} %copy.68), calls=%async_computation.7 | async-start | bytes 2097152 | tf_op jit(solution)/shard_map/all_to_all | solution.py:51
Sparse Core Ops, SparseCore 0:
  335.9 32.7 all-gather.1
where the time goes:
time: 449 us; the launch traced here: 442 us
  other arithmetic  205 us (46%)
  local copies, waits for them, and re-layouts  84.3 us (19%)
  blocking collectives  75.4 us (17%)
  waiting for transfers between devices  40.3 us (9%)
  starting transfers between devices  22.9 us (5%)
  between operations  14.2 us (3%)
    unnamed x3, other arithmetic  161 us
    unnamed x14, local copies, waits for them, and re-layouts  32.5 us
    all_to_all x1, blocking collectives, per_device(): lax.all_to_all(sectioned, 'fsdp', split_axis=2, concat_axis=2, tiled=True)  32.5 us
    all_to_all x1, blocking collectives, per_device(): lax.all_to_all(going, 'fsdp', split_axis=3, concat_axis=0, tiled=True)  27.8 us
    convert_element_type x1, local copies, waits for them, and re-layouts, per_device(): (block_grouped / block_scales.astype(jnp.float32)[:, :, None]).astype(jnp...  27 us
    all_to_all x1, waiting for transfers between devices, per_device(): lax.all_to_all(going, 'fsdp', split_axis=2, concat_axis=2, tiled=True)  20.9 us
    convert_element_type x1, other arithmetic, dequantise(): integer_levels.astype(jnp.float32).reshape(block_scales.shape + (QBLOCK,))  17.6 us
    all_to_all x1, waiting for transfers between devices, per_device(): lax.all_to_all(levels_local, 'replica', split_axis=2, concat_axis=0, tile...  16.3 us
  transfers between devices with their start and end apart: 6, of which 3 were waited for; matrix products, arithmetic and copies ran while one was open for 61% of the time, Pallas kernels for 0%

commit v1 on v0

v1 whole, which is shorter than its diff:
```python
import functools

import jax
import jax.numpy as jnp
from jax import lax
from jax.experimental import pallas as pl
from jax.experimental.pallas import tpu as pltpu
from jax.sharding import PartitionSpec as P

LANES = 128
LEARN_RATE = 0.7
MOMENTUM_COEF = 0.9
MESH = pl.DeviceIdType.MESH


def sync_kernel(
    replicas, group, per,
    local, base, mom, gathered, avg_home,
    loc_recv, base_own, m_recv, u_own, avg_own,
    rs_send, rs_recv, m_send_sem, m_recv_sem, ag_send, ag_recv, h_send, h_recv, own_sem, base_sem, out_sem,
):
    r = lax.axis_index("replica")
    f = lax.axis_index("fsdp")
    rows, cols = local.shape
    quarter = cols // replicas
    piece = mom.shape[1]
    width = piece // per
    chunks = group * per
    line = f // group
    sub = f % group
    diagonal = line == r

    def span(start):
        return pl.ds(pl.multiple_of(start, LANES), width)

    def side(k):
        return r * group + k

    own, own_base = [], []
    for c in range(chunks):
        at = span(r * quarter + c * width)
        own.append(pltpu.make_async_copy(local.at[:, at], loc_recv.at[0, :, pl.ds(c * width, width)], own_sem.at[c]))
        own_base.append(pltpu.make_async_copy(base.at[:, at], base_own.at[:, pl.ds(c * width, width)], base_sem.at[c]))
    for c in range(chunks):
        own[c].start()
        own_base[c].start()

    barrier = pltpu.get_barrier_semaphore()
    for d in range(1, replicas):
        pl.semaphore_signal(barrier, inc=1, device_id={"replica": r ^ d}, device_id_type=MESH)
    for k in range(group):
        @pl.when(jnp.logical_or(line != r, sub != k))
        def _():
            pl.semaphore_signal(barrier, inc=1, device_id={"replica": line, "fsdp": side(k)}, device_id_type=MESH)
    pl.semaphore_wait(barrier, replicas - 1 + group - diagonal.astype(jnp.int32))

    def m_copies(k, i):
        src = mom.at[pl.ds(k * rows, rows), pl.ds(i * width, width)]
        dst = m_recv.at[:, span(sub * piece + i * width)]
        arrived = m_recv_sem.at[sub * per + i]
        return (
            pltpu.make_async_remote_copy(
                src_ref=src, dst_ref=dst, send_sem=m_send_sem.at[k * per + i], recv_sem=arrived,
                device_id={"replica": line, "fsdp": side(k)}, device_id_type=MESH),
            pltpu.make_async_copy(src, dst, arrived),
        )

    def h_copies(c):
        j, i = divmod(c, per)
        src = avg_own.at[:, pl.ds(c * width, width)]
        dst = avg_home.at[pl.ds(pl.multiple_of(sub * rows, rows), rows), pl.ds(i * width, width)]
        arrived = h_recv.at[sub * per + i]
        return (
            pltpu.make_async_remote_copy(
                src_ref=src, dst_ref=dst, send_sem=h_send.at[c], recv_sem=arrived,
                device_id={"replica": line, "fsdp": side(j)}, device_id_type=MESH),
            pltpu.make_async_copy(src, dst, arrived),
        )

    def elsewhere(k):
        return jnp.logical_or(line != r, sub != k)

    def start(pair, k):
        far, near = pair
        pl.when(elsewhere(k))(far.start)
        pl.when(jnp.logical_not(elsewhere(k)))(near.start)

    def wait_sent(pair, k):
        pl.when(elsewhere(k))(pair[0].wait_send)

    def rs_copy(d, c):
        t = r ^ d
        return pltpu.make_async_remote_copy(
            src_ref=local.at[:, span(t * quarter + c * width)],
            dst_ref=loc_recv.at[d, :, pl.ds(c * width, width)],
            send_sem=rs_send.at[d - 1, c], recv_sem=rs_recv.at[d - 1, c],
            device_id={"replica": t}, device_id_type=MESH)

    def ag_copy(d, c):
        return pltpu.make_async_remote_copy(
            src_ref=u_own.at[:, pl.ds(c * width, width)],
            dst_ref=gathered.at[:, span(r * quarter + c * width)],
            send_sem=ag_send.at[d - 1, c], recv_sem=ag_recv.at[d - 1, c],
            device_id={"replica": r ^ d}, device_id_type=MESH)

    order = list(range(replicas - 1, 0, -1))
    for i in range(per):
        for k in range(group):
            start(m_copies(k, i), k)
    for c in range(chunks):
        for d in order:
            rs_copy(d, c).start()

    def wait_bytes(ref, sem):
        pltpu.make_async_copy(ref, ref, sem).wait()

    outs = []
    for c in range(chunks):
        here = pl.ds(c * width, width)
        own[c].wait()
        own_base[c].wait()
        for d in order:
            rs_copy(d, c).wait_recv()
        wait_bytes(m_recv.at[:, here], m_recv_sem.at[c])
        total = loc_recv[0, :, here].astype(jnp.float32)
        for d in range(1, replicas):
            total = total + loc_recv[d, :, here].astype(jnp.float32)
        average = base_own[:, here] - total * (1.0 / replicas)
        new = MOMENTUM_COEF * m_recv[:, here].astype(jnp.float32) + average
        update = LEARN_RATE * (average + MOMENTUM_COEF * new)
        u_own[:, here] = update.astype(jnp.bfloat16)
        avg_own[:, here] = average.astype(jnp.bfloat16)
        for d in order:
            ag_copy(d, c).start()
        start(h_copies(c), c // per)
        out = pltpu.make_async_copy(u_own.at[:, here], gathered.at[:, span(r * quarter + c * width)], out_sem.at[c])
        out.start()
        outs.append(out)

    for c in range(chunks):
        for d in order:
            ag_copy(d, c).wait_recv()
    for k in range(group):
        for i in range(per):
            wait_bytes(avg_home.at[pl.ds(k * rows, rows), pl.ds(i * width, width)], h_recv.at[k * per + i])
    for c in range(chunks):
        outs[c].wait()
        for d in order:
            rs_copy(d, c).wait_send()
            ag_copy(d, c).wait_send()
        wait_sent(h_copies(c), c // per)
    for i in range(per):
        for k in range(group):
            wait_sent(m_copies(k, i), k)


def per_device(local_weights, base_weights, momentum):
    rows, cols = base_weights.shape
    replicas = lax.axis_size("replica")
    group = lax.axis_size("fsdp") // replicas
    piece = momentum.shape[1]
    per = 2 if piece % (2 * LANES) == 0 else 1
    chunks = group * per
    quarter = cols // replicas
    dma = pltpu.SemaphoreType.DMA
    gathered, avg_home = pl.pallas_call(
        functools.partial(sync_kernel, replicas, group, per),
        out_shape=(
            jax.ShapeDtypeStruct((rows, cols), jnp.bfloat16),
            jax.ShapeDtypeStruct(momentum.shape, jnp.bfloat16),
        ),
        in_specs=[pl.BlockSpec(memory_space=pl.ANY)] * 3,
        out_specs=(pl.BlockSpec(memory_space=pl.ANY),) * 2,
        scratch_shapes=[
            pltpu.VMEM((replicas, rows, quarter), jnp.bfloat16),
            pltpu.VMEM((rows, quarter), jnp.float32),
            pltpu.VMEM((rows, quarter), jnp.bfloat16),
            pltpu.VMEM((rows, quarter), jnp.bfloat16),
            pltpu.VMEM((rows, quarter), jnp.bfloat16),
            dma((replicas - 1, chunks)), dma((replicas - 1, chunks)),
            dma((chunks,)), dma((chunks,)),
            dma((replicas - 1, chunks)), dma((replicas - 1, chunks)),
            dma((chunks,)), dma((chunks,)),
            dma((chunks,)), dma((chunks,)), dma((chunks,)),
        ],
        compiler_params=pltpu.CompilerParams(collective_id=0, has_side_effects=True),
    )(local_weights[0], base_weights, momentum.astype(jnp.bfloat16))
    new_weights = base_weights - gathered.astype(jnp.float32)
    new_momentum = MOMENTUM_COEF * momentum + avg_home.astype(jnp.float32)
    return new_weights, new_momentum


def solution(mesh):
    return jax.shard_map(
        per_device,
        mesh=mesh,
        in_specs=(P("replica", "fsdp", None), P("fsdp", None), P("replica", "fsdp")),
        out_specs=(P("fsdp", None), P("replica", "fsdp")),
        check_vma=False,
    )
```

time: 449 us -> 92.1 us (0.21)
  the two profiles are of different devices: /device:TPU:7 before, /device:TPU:0 now
where the time goes in v1:
time: 92.1 us; the launch traced here: 92 us
  Pallas kernels  83.5 us (91%)
  other arithmetic  7.86 us (9%)
    pallas_call x1, Pallas kernels, per_device(): pl.pallas_call(functools.partial(sync_kernel, replicas, group, per), out_...  83.5 us
    sub x1, other arithmetic, per_device(): new_weights = base_weights - gathered.astype(jnp.float32)  4.85 us
    convert_element_type x1, other arithmetic, per_device(): momentum.astype(jnp.bfloat16)  1.99 us

profile of v1, /device:TPU:0, one launch (start us, length us, event | category | flops | bytes accessed | tf_op | source)
XLA Modules:
  0.0 92.0 jit_solution(5490632772673003992)
XLA Ops:
  0.6 2.0 %convert_element_type.9.mom = bf16[64,3584]{1,0:T(8,128)(2,1)} convert(f32[64,3584]{1,0:T(8,128)} %param.5) | non-fusion elementwise | flops 229376 | bytes 1376256 | tf_op jit(solution)/shard_map/convert_element_type | solution.py:187
  2.6 83.5 %shard_map.50 = (bf16[32,28672]{1,0:T(8,128)(2,1)}, bf16[64,3584]{1,0:T(8,128)(2,1)}) custom-call(bf16[32,28672]{1,0:T(8,128)(2,1)} %bitcast.1, f32[32,28672]{1,0:T(8,128)} %base.1, bf16[64,3584]{1,0:T(8,128)(2,1)} %convert_element_type.9.mom), custom_call_target="tpu_custom_call" | custom-call | tf_op jit(solution)/shard_map/pallas_call | solution.py:166
  86.1 0.0 copy-start
  86.1 0.0 copy-start.1
  86.1 4.8 %convert_subtract_fusion = f32[32,28672]{1,0:T(8,128)} fusion(f32[32,28672]{1,0:T(8,128)} %base.1, bf16[32,28672]{1,0:T(8,128)(2,1)} %get-tuple-element.4), kind=kLoop, calls=%fused_computation | loop fusion | flops 1835008 | bytes 9175040 | tf_op jit(solution)/shard_map/sub | solution.py:188
  91.0 0.0 copy-done
  91.0 0.0 copy-done.1
  91.0 1.0 %convert_add_fusion = f32[64,3584]{1,0:T(8,128)} fusion(bf16[64,3584]{1,0:T(8,128)(2,1)S(1)} %copy-done.1, f32[64,3584]{1,0:T(8,128)S(1)} %copy-done), kind=kLoop, calls=%fused_computation.1 | loop fusion | flops 688128 | bytes 2293760 | tf_op jit(solution)/shard_map/add | solution.py:189
Async XLA Ops:
  86.1 4.9 %copy-start = (f32[64,3584]{1,0:T(8,128)S(1)}, f32[64,3584]{1,0:T(8,128)}, u32[]{:S(2)}) copy-start(f32[64,3584]{1,0:T(8,128)} %param.5) | copy-start | bytes 2752516
  86.1 4.9 %copy-start.1 = (bf16[64,3584]{1,0:T(8,128)(2,1)S(1)}, bf16[64,3584]{1,0:T(8,128)(2,1)}, u32[]{:S(2)}) copy-start(bf16[64,3584]{1,0:T(8,128)(2,1)} %get-tuple-element.5) | copy-start | bytes 1376260

commit v2 on v0

v2 whole, which is shorter than its diff:
```python
import functools

import jax
import jax.numpy as jnp
from jax import lax
from jax.experimental import pallas as pl
from jax.experimental.pallas import tpu as pltpu
from jax.sharding import PartitionSpec as P

LANES = 128
LEARN_RATE = 0.7
MOMENTUM_COEF = 0.9
MESH = pl.DeviceIdType.MESH
AHEAD = 2
LAG = 2


def sync_kernel(
    replicas, shards, per,
    local, base, mom, gathered, u_home,
    base_vm, loc_vm, m_recv, fold, loc_recv, u_own, total,
    rs_send, rs_recv, m_send, m_arrived, ag_send, ag_recv, h_send, h_recv, load_sem, out_sem,
):
    r = lax.axis_index("replica")
    f = lax.axis_index("fsdp")
    group = shards // replicas
    rows, cols = local.shape
    quarter = cols // replicas
    piece = mom.shape[1]
    width = piece // per
    line = f // group
    sub = f % group
    hub = line == r
    fold_coef = replicas * MOMENTUM_COEF * MOMENTUM_COEF / (1.0 + MOMENTUM_COEF)
    steps = [(i, j) for i in range(per) for j in range(group)]

    def span(start):
        return pl.ds(pl.multiple_of(start, LANES), width)

    load_local = pltpu.make_async_copy(local, loc_vm, load_sem.at[0])
    load_base = pltpu.make_async_copy(base, base_vm, load_sem.at[1])
    load_local.start()
    load_base.start()

    barrier = pltpu.get_barrier_semaphore()
    for d in range(1, replicas):
        pl.semaphore_signal(barrier, inc=1, device_id={"replica": r ^ d}, device_id_type=MESH)
    for e in range(1, shards):
        other = f ^ e

        @pl.when(jnp.logical_or(hub, other // group == r))
        def _():
            pl.semaphore_signal(barrier, inc=1, device_id={"fsdp": other}, device_id_type=MESH)

    pl.semaphore_wait(barrier, replicas - 1 + jnp.where(hub, shards - 1, group))

    def m_far(k, i):
        return pltpu.make_async_remote_copy(
            src_ref=mom.at[pl.ds(k * rows, rows), pl.ds(i * width, width)],
            dst_ref=m_recv.at[:, span(f * piece + i * width)],
            send_sem=m_send.at[k * per + i], recv_sem=m_arrived.at[f * per + i],
            device_id={"fsdp": r * group + k}, device_id_type=MESH)

    def m_near(k, i):
        return pltpu.make_async_copy(
            mom.at[pl.ds(k * rows, rows), pl.ds(i * width, width)],
            m_recv.at[:, span(f * piece + i * width)], m_arrived.at[f * per + i])

    def rs_copy(d, i, j, source):
        c = j * per + i
        return pltpu.make_async_remote_copy(
            src_ref=source.at[:, span((r ^ d) * quarter + c * width)],
            dst_ref=loc_recv.at[d - 1, :, pl.ds(c * width, width)],
            send_sem=rs_send.at[d - 1, c], recv_sem=rs_recv.at[d - 1, c],
            device_id={"replica": r ^ d}, device_id_type=MESH)

    def ag_copy(d, i, j):
        c = j * per + i
        return pltpu.make_async_remote_copy(
            src_ref=u_own.at[:, pl.ds(c * width, width)],
            dst_ref=gathered.at[:, span(r * quarter + c * width)],
            send_sem=ag_send.at[d - 1, c], recv_sem=ag_recv.at[d - 1, c],
            device_id={"replica": r ^ d}, device_id_type=MESH)

    def h_source(d, i, j):
        c = j * per + i
        if d == 0:
            return u_own.at[:, pl.ds(c * width, width)]
        return gathered.at[:, span((r ^ d) * quarter + c * width)]

    def h_target(i):
        return u_home.at[pl.ds(pl.multiple_of(sub * rows, rows), rows), pl.ds(i * width, width)]

    def h_far(d, i, j):
        return pltpu.make_async_remote_copy(
            src_ref=h_source(d, i, j), dst_ref=h_target(i),
            send_sem=h_send.at[d, j * per + i], recv_sem=h_recv.at[sub * per + i],
            device_id={"fsdp": (r ^ d) * group + j}, device_id_type=MESH)

    def h_near(i, j):
        return pltpu.make_async_copy(h_source(0, i, j), h_target(i), h_recv.at[sub * per + i])

    def wait_bytes(ref, sem):
        pltpu.make_async_copy(ref, ref, sem).wait()

    order = list(range(replicas - 1, 0, -1))

    def send_local(i, j):
        @pl.when(jnp.logical_not(hub))
        def _():
            for d in order:
                rs_copy(d, i, j, local).start()

    def send_fold(i, j):
        @pl.when(hub)
        def _():
            for d in [0] + order[::-1]:
                side = (r ^ d) * group + j
                at = span(side * piece + i * width)
                wait_bytes(m_recv.at[:, at], m_arrived.at[side * per + i])
                if d:
                    delta = base_vm[:, at] - loc_vm[:, at].astype(jnp.float32)
                    fold[:, at] = (delta + fold_coef * m_recv[:, at].astype(jnp.float32)).astype(jnp.bfloat16)
                    rs_copy(d, i, j, fold).start()

    def reduce(i, j):
        c = j * per + i
        here = pl.ds(c * width, width)
        at = span(r * quarter + c * width)
        own_base = base_vm[:, at]
        total[...] = own_base - loc_vm[:, at].astype(jnp.float32)

        @pl.when(hub)
        def _():
            total[...] += fold_coef * m_recv[:, at].astype(jnp.float32)

        for d in order:
            rs_copy(d, i, j, local).wait_recv()
        summed = total[...]
        for d in range(1, replicas):
            came = loc_recv[d - 1, :, here].astype(jnp.float32)
            summed = summed + jnp.where((r ^ d) == line, came, own_base - came)
        scale = LEARN_RATE * (1.0 + MOMENTUM_COEF) / replicas
        u_own[:, here] = (scale * summed).astype(jnp.bfloat16)
        for d in order:
            ag_copy(d, i, j).start()

        @pl.when(jnp.logical_and(hub, sub != j))
        def _():
            h_far(0, i, j).start()

        @pl.when(jnp.logical_and(hub, sub == j))
        def _():
            h_near(i, j).start()

        out_copy(i, j).start()

    def out_copy(i, j):
        c = j * per + i
        return pltpu.make_async_copy(
            u_own.at[:, pl.ds(c * width, width)], gathered.at[:, span(r * quarter + c * width)], out_sem.at[c])

    def give_back(i, j):
        for d in order[::-1]:
            ag_copy(d, i, j).wait_recv()

            @pl.when(hub)
            def _():
                h_far(d, i, j).start()

    for i in range(per):
        for k in range(group):
            away = f != r * group + k

            @pl.when(away)
            def _():
                m_far(k, i).start()

            @pl.when(jnp.logical_not(away))
            def _():
                m_near(k, i).start()

    for s in range(min(AHEAD, len(steps))):
        send_local(*steps[s])
    load_local.wait()
    load_base.wait()
    for s in range(len(steps) + LAG):
        if s + AHEAD < len(steps):
            send_local(*steps[s + AHEAD])
        if s < len(steps):
            send_fold(*steps[s])
            reduce(*steps[s])
        if s >= LAG:
            give_back(*steps[s - LAG])

    for k in range(group):
        for i in range(per):
            wait_bytes(u_home.at[pl.ds(k * rows, rows), pl.ds(i * width, width)], h_recv.at[k * per + i])

            @pl.when(f != r * group + k)
            def _():
                m_far(k, i).wait_send()

    for i, j in steps:
        out_copy(i, j).wait()
        for d in order:
            rs_copy(d, i, j, local).wait_send()
            ag_copy(d, i, j).wait_send()

        @pl.when(hub)
        def _():
            for d in order:
                h_far(d, i, j).wait_send()

        @pl.when(jnp.logical_and(hub, sub != j))
        def _():
            h_far(0, i, j).wait_send()


def per_device(local_weights, base_weights, momentum):
    rows, cols = base_weights.shape
    replicas = lax.axis_size("replica")
    shards = lax.axis_size("fsdp")
    group = shards // replicas
    piece = momentum.shape[1]
    per = next(n for n in (4, 2, 1) if piece % (n * LANES) == 0)
    chunks = group * per
    quarter = cols // replicas
    dma = pltpu.SemaphoreType.DMA
    gathered, u_home = pl.pallas_call(
        functools.partial(sync_kernel, replicas, shards, per),
        out_shape=(
            jax.ShapeDtypeStruct((rows, cols), jnp.bfloat16),
            jax.ShapeDtypeStruct(momentum.shape, jnp.bfloat16),
        ),
        in_specs=[pl.BlockSpec(memory_space=pl.ANY)] * 3,
        out_specs=(pl.BlockSpec(memory_space=pl.ANY),) * 2,
        scratch_shapes=[
            pltpu.VMEM((rows, cols), jnp.float32),
            pltpu.VMEM((rows, cols), jnp.bfloat16),
            pltpu.VMEM((rows, cols), jnp.bfloat16),
            pltpu.VMEM((rows, cols), jnp.bfloat16),
            pltpu.VMEM((replicas - 1, rows, quarter), jnp.bfloat16),
            pltpu.VMEM((rows, quarter), jnp.bfloat16),
            pltpu.VMEM((rows, piece // per), jnp.float32),
            dma((replicas - 1, chunks)), dma((replicas - 1, chunks)),
            dma((group * per,)), dma((shards * per,)),
            dma((replicas - 1, chunks)), dma((replicas - 1, chunks)),
            dma((replicas, chunks)), dma((group * per,)),
            dma((2,)), dma((chunks,)),
        ],
        compiler_params=pltpu.CompilerParams(
            collective_id=0, has_side_effects=True, vmem_limit_bytes=48 * 1024 * 1024),
    )(local_weights[0], base_weights, momentum.astype(jnp.bfloat16))
    new_weights = base_weights - gathered.astype(jnp.float32)
    new_momentum = (MOMENTUM_COEF * momentum + unscaled(u_home)) / (1.0 + MOMENTUM_COEF)
    return new_weights, new_momentum


def unscaled(update):
    return update.astype(jnp.float32) / LEARN_RATE


def solution(mesh):
    return jax.shard_map(
        per_device,
        mesh=mesh,
        in_specs=(P("replica", "fsdp", None), P("fsdp", None), P("replica", "fsdp")),
        out_specs=(P("fsdp", None), P("replica", "fsdp")),
        check_vma=False,
    )
```

time: 449 us -> 83.9 us (0.19); the launches traced: 442 us -> 83.7 us
  other arithmetic: 205 us -> 4.46 us
  local copies, waits for them, and re-layouts: 84.3 us -> 1.5 us
  Pallas kernels: 0 us -> 77.1 us
  blocking collectives: 75.4 us -> 0 us
  waiting for transfers between devices: 40.3 us -> 0 us
  starting transfers between devices: 22.9 us -> 0 us
  between operations: 14.2 us -> 0.67 us
    unnamed x3 -> x0, other arithmetic: 161 us -> none
    pallas_call x0 -> x1, Pallas kernels: none -> 77.1 us  [per_device(): pl.pallas_call(functools.partial(sync_kernel, replicas, shards, per), out...]
    all_to_all x3 -> x0, blocking collectives: 75.4 us -> none  [the longest x1 32.5 us: per_device(): lax.all_to_all(sectioned, 'fsdp', split_axis=2, concat_axis=2, tiled=True)]
    all_to_all x5 -> x0, waiting for transfers between devices: 40.3 us -> none  [the longest x1 20.9 us: per_device(): lax.all_to_all(going, 'fsdp', split_axis=2, concat_axis=2, tiled=True)]
    unnamed x14 -> x6, local copies, waits for them, and re-layouts: 32.5 us -> 1.5 us
    convert_element_type x2 -> x0, local copies, waits for them, and re-layouts: 27.1 us -> none  [the longest x1 27 us: per_device(): (block_grouped / block_scales.astype(jnp.float32)[:, :, None]).astype(jnp...]
    all_to_all x5 -> x0, starting transfers between devices: 22.9 us -> none  [the longest x1 5.35 us: per_device(): lax.all_to_all(going, 'fsdp', split_axis=2, concat_axis=2, tiled=True)]
    convert_element_type x4 -> x1, other arithmetic: 21.3 us -> 1.23 us  [per_device(): momentum.astype(jnp.bfloat16)]
  transfers between devices with their start and end apart: 6 -> 0, of which waited for: 3 -> 0; matrix products, arithmetic and copies ran while one was open for 61% -> 0% of each run, Pallas kernels for 0% -> 0%
where the time goes in v2:
time: 83.9 us; the launch traced here: 83.7 us
  Pallas kernels  77.1 us (92%)
  other arithmetic  4.46 us (5%)
  local copies, waits for them, and re-layouts  1.5 us (2%)
    pallas_call x1, Pallas kernels, per_device(): pl.pallas_call(functools.partial(sync_kernel, replicas, shards, per), out...  77.1 us
    sub x1, other arithmetic, per_device(): new_weights = base_weights - gathered.astype(jnp.float32)  2.14 us

profile of v2, /device:TPU:7, one launch (start us, length us, event | category | flops | bytes accessed | tf_op | source)
XLA Modules:
  0.0 83.7 jit_solution(17888159260386097227)
XLA Ops:
  0.6 1.2 %convert_element_type.9.mom = bf16[64,3584]{1,0:T(8,128)(2,1)S(1)} convert(f32[64,3584]{1,0:T(8,128)} %param.5) | non-fusion elementwise | flops 229376 | bytes 1376256 | tf_op jit(solution)/shard_map/convert_element_type | solution.py:254
  1.9 0.0 copy-start
  1.9 1.5 %copy-done = bf16[1,32,28672]{2,1,0:T(8,128)(2,1)S(1)} copy-done((bf16[1,32,28672]{2,1,0:T(8,128)(2,1)S(1)}, bf16[1,32,28672]{2,1,0:T(8,128)(2,1)}, u32[]{:S(2)}) %copy-start) | copy-done | bytes 1835032
  3.4 0.0 copy-start.1
  3.4 77.1 %shard_map.50 = (bf16[32,28672]{1,0:T(8,128)(2,1)S(1)}, bf16[64,3584]{1,0:T(8,128)(2,1)S(1)}) custom-call(bf16[32,28672]{1,0:T(8,128)(2,1)S(1)} %bitcast.1, f32[32,28672]{1,0:T(8,128)} %base.1, bf16[64,3584]{1,0:T(8,128)(2,1)S(1)} %convert_element_type.9.mom), custom_call_target="tpu_custom_call" | custom-call | tf_op jit(solution)/shard_map/pallas_call | solution.py:230
  80.4 0.0 copy-done.1
  80.4 0.0 copy-start.2
  80.5 2.1 %convert_subtract_fusion = f32[32,28672]{1,0:T(8,128)} fusion(f32[32,28672]{1,0:T(8,128)S(1)} %copy-done.1, bf16[32,28672]{1,0:T(8,128)(2,1)S(1)} %get-tuple-element.4), kind=kLoop, calls=%fused_computation | loop fusion | flops 1835008 | bytes 9175040 | tf_op jit(solution)/shard_map/sub | solution.py:255
  82.6 0.0 copy-done.2
  82.6 1.1 %add_multiply_fusion = f32[64,3584]{1,0:T(8,128)} fusion(bf16[64,3584]{1,0:T(8,128)(2,1)S(1)} %get-tuple-element.5, f32[64,3584]{1,0:T(8,128)S(1)} %copy-done.2), kind=kLoop, calls=%fused_computation.1 | loop fusion | flops 1146880 | bytes 2293760 | tf_op jit(solution)/shard_map/div | solution.py:256
Async XLA Ops:
  1.9 1.5 %copy-start = (bf16[1,32,28672]{2,1,0:T(8,128)(2,1)S(1)}, bf16[1,32,28672]{2,1,0:T(8,128)(2,1)}, u32[]{:S(2)}) copy-start(bf16[1,32,28672]{2,1,0:T(8,128)(2,1)} %param.3) | copy-start | bytes 5505028
  3.4 77.1 %copy-start.1 = (f32[32,28672]{1,0:T(8,128)S(1)}, f32[32,28672]{1,0:T(8,128)}, u32[]{:S(2)}) copy-start(f32[32,28672]{1,0:T(8,128)} %base.1) | copy-start | bytes 11010052
  80.4 2.2 %copy-start.2 = (f32[64,3584]{1,0:T(8,128)S(1)}, f32[64,3584]{1,0:T(8,128)}, u32[]{:S(2)}) copy-start(f32[64,3584]{1,0:T(8,128)} %param.5) | copy-start | bytes 2752516

commit v3 on v2

--- a/solution.py
+++ b/solution.py
@@ -17,8 +17,8 @@
 
 def sync_kernel(
     replicas, shards, per,
-    local, base, mom, gathered, u_home,
-    base_vm, loc_vm, m_recv, fold, loc_recv, u_own, total,
+    local, base, mom_full, gathered, u_home,
+    base_vm, loc_vm, mom_vm, mom, m_recv, fold, loc_recv, u_own, total,
     rs_send, rs_recv, m_send, m_arrived, ag_send, ag_recv, h_send, h_recv, load_sem, out_sem,
 ):
     r = lax.axis_index("replica")
@@ -41,6 +41,8 @@
     load_base = pltpu.make_async_copy(base, base_vm, load_sem.at[1])
     load_local.start()
     load_base.start()
+    load_mom = pltpu.make_async_copy(mom_full, mom_vm, load_sem.at[2])
+    load_mom.start()
 
     barrier = pltpu.get_barrier_semaphore()
     for d in range(1, replicas):
@@ -52,6 +54,8 @@
         def _():
             pl.semaphore_signal(barrier, inc=1, device_id={"fsdp": other}, device_id_type=MESH)
 
+    load_mom.wait()
+    mom[...] = mom_vm[...].astype(jnp.bfloat16)
     pl.semaphore_wait(barrier, replicas - 1 + jnp.where(hub, shards - 1, group))
 
     def m_far(k, i):
@@ -168,7 +172,7 @@
             def _():
                 h_far(d, i, j).start()
 
-    for i in range(per):
+    def send_momentum(i):
         for k in range(group):
             away = f != r * group + k
 
@@ -181,10 +185,14 @@
                 m_near(k, i).start()
 
     for s in range(min(AHEAD, len(steps))):
+        if s < per:
+            send_momentum(s)
         send_local(*steps[s])
     load_local.wait()
     load_base.wait()
     for s in range(len(steps) + LAG):
+        if s % group == 0 and AHEAD <= s // group + AHEAD < per:
+            send_momentum(s // group + AHEAD)
         if s + AHEAD < len(steps):
             send_local(*steps[s + AHEAD])
         if s < len(steps):
@@ -238,6 +246,8 @@
         scratch_shapes=[
             pltpu.VMEM((rows, cols), jnp.float32),
             pltpu.VMEM((rows, cols), jnp.bfloat16),
+            pltpu.VMEM(momentum.shape, jnp.float32),
+            pltpu.VMEM(momentum.shape, jnp.bfloat16),
             pltpu.VMEM((rows, cols), jnp.bfloat16),
             pltpu.VMEM((rows, cols), jnp.bfloat16),
             pltpu.VMEM((replicas - 1, rows, quarter), jnp.bfloat16),
@@ -247,11 +257,11 @@
             dma((group * per,)), dma((shards * per,)),
             dma((replicas - 1, chunks)), dma((replicas - 1, chunks)),
             dma((replicas, chunks)), dma((group * per,)),
-            dma((2,)), dma((chunks,)),
+            dma((3,)), dma((chunks,)),
         ],
         compiler_params=pltpu.CompilerParams(
             collective_id=0, has_side_effects=True, vmem_limit_bytes=48 * 1024 * 1024),
-    )(local_weights[0], base_weights, momentum.astype(jnp.bfloat16))
+    )(local_weights[0], base_weights, momentum)
     new_weights = base_weights - gathered.astype(jnp.float32)
     new_momentum = (MOMENTUM_COEF * momentum + unscaled(u_home)) / (1.0 + MOMENTUM_COEF)
     return new_weights, new_momentum

time: 83.9 us -> 81.6 us (0.973)
  Pallas kernels: 77.1 us -> 74.8 us
  other arithmetic: 4.46 us -> 3.23 us
  local copies, waits for them, and re-layouts: 1.5 us -> 2.67 us
    pallas_call x1, Pallas kernels: 77.1 us -> 74.8 us  [per_device(): pl.pallas_call(functools.partial(sync_kernel, replicas, shards, per), out...]
    convert_element_type x1 -> x0, other arithmetic: 1.23 us -> none  [per_device(): momentum.astype(jnp.bfloat16)]
    unnamed x6, local copies, waits for them, and re-layouts: 1.5 us -> 2.67 us
where the time goes in v3:
time: 81.6 us; the launch traced here: 81.4 us
  Pallas kernels  74.8 us (92%)
  other arithmetic  3.23 us (4%)
  local copies, waits for them, and re-layouts  2.67 us (3%)
    pallas_call x1, Pallas kernels, per_device(): pl.pallas_call(functools.partial(sync_kernel, replicas, shards, per), out...  74.8 us
    unnamed x6, local copies, waits for them, and re-layouts  2.67 us
    sub x1, other arithmetic, per_device(): new_weights = base_weights - gathered.astype(jnp.float32)  2.14 us

profile of v3, /device:TPU:7, one launch (start us, length us, event | category | flops | bytes accessed | tf_op | source)
XLA Modules:
  0.0 81.4 jit_solution(1077371310307256509)
XLA Ops:
  0.6 0.0 copy-start
  0.6 1.2 %copy-done = f32[64,3584]{1,0:T(8,128)S(1)} copy-done((f32[64,3584]{1,0:T(8,128)S(1)}, f32[64,3584]{1,0:T(8,128)}, u32[]{:S(2)}) %copy-start) | copy-done | bytes 917528
  1.8 0.0 copy-start.1
  1.8 1.5 %copy-done.1 = bf16[1,32,28672]{2,1,0:T(8,128)(2,1)S(1)} copy-done((bf16[1,32,28672]{2,1,0:T(8,128)(2,1)S(1)}, bf16[1,32,28672]{2,1,0:T(8,128)(2,1)}, u32[]{:S(2)}) %copy-start.1) | copy-done | bytes 1835032
  3.3 0.0 copy-start.2
  3.3 74.8 %shard_map.50 = (bf16[32,28672]{1,0:T(8,128)(2,1)S(1)}, bf16[64,3584]{1,0:T(8,128)(2,1)S(1)}) custom-call(bf16[32,28672]{1,0:T(8,128)(2,1)S(1)} %bitcast.1, f32[32,28672]{1,0:T(8,128)} %base.1, f32[64,3584]{1,0:T(8,128)S(1)} %copy-done), custom_call_target="tpu_custom_call" | custom-call | tf_op jit(solution)/shard_map/pallas_call | solution.py:238
  78.2 0.0 copy-done.2
  78.2 2.1 %convert_subtract_fusion = f32[32,28672]{1,0:T(8,128)} fusion(f32[32,28672]{1,0:T(8,128)S(1)} %copy-done.2, bf16[32,28672]{1,0:T(8,128)(2,1)S(1)} %get-tuple-element.4), kind=kLoop, calls=%fused_computation | loop fusion | flops 1835008 | bytes 9175040 | tf_op jit(solution)/shard_map/sub | solution.py:265
  80.3 1.1 %add_multiply_fusion = f32[64,3584]{1,0:T(8,128)} fusion(bf16[64,3584]{1,0:T(8,128)(2,1)S(1)} %get-tuple-element.5, f32[64,3584]{1,0:T(8,128)S(1)} %copy-done), kind=kLoop, calls=%fused_computation.1 | loop fusion | flops 1146880 | bytes 2293760 | tf_op jit(solution)/shard_map/div | solution.py:266
Async XLA Ops:
  0.6 1.2 %copy-start = (f32[64,3584]{1,0:T(8,128)S(1)}, f32[64,3584]{1,0:T(8,128)}, u32[]{:S(2)}) copy-start(f32[64,3584]{1,0:T(8,128)} %mom_full.1) | copy-start | bytes 2752516
  1.8 1.5 %copy-start.1 = (bf16[1,32,28672]{2,1,0:T(8,128)(2,1)S(1)}, bf16[1,32,28672]{2,1,0:T(8,128)(2,1)}, u32[]{:S(2)}) copy-start(bf16[1,32,28672]{2,1,0:T(8,128)(2,1)} %param.3) | copy-start | bytes 5505028
  3.3 74.8 %copy-start.2 = (f32[32,28672]{1,0:T(8,128)S(1)}, f32[32,28672]{1,0:T(8,128)}, u32[]{:S(2)}) copy-start(f32[32,28672]{1,0:T(8,128)} %base.1) | copy-start | bytes 11010052

commit v4 on v3

--- a/solution.py
+++ b/solution.py
@@ -11,8 +11,9 @@
 LEARN_RATE = 0.7
 MOMENTUM_COEF = 0.9
 MESH = pl.DeviceIdType.MESH
-AHEAD = 2
-LAG = 2
+AHEAD = 3
+LAG = 3
+M_AHEAD = 1
 
 
 def sync_kernel(
@@ -184,15 +185,16 @@
             def _():
                 m_near(k, i).start()
 
-    for s in range(min(AHEAD, len(steps))):
-        if s < per:
+    for s in range(max(AHEAD, M_AHEAD)):
+        if s < min(M_AHEAD, per):
             send_momentum(s)
-        send_local(*steps[s])
+        if s < min(AHEAD, len(steps)):
+            send_local(*steps[s])
     load_local.wait()
     load_base.wait()
     for s in range(len(steps) + LAG):
-        if s % group == 0 and AHEAD <= s // group + AHEAD < per:
-            send_momentum(s // group + AHEAD)
+        if s % group == 0 and s // group + M_AHEAD < per:
+            send_momentum(s // group + M_AHEAD)
         if s + AHEAD < len(steps):
             send_local(*steps[s + AHEAD])
         if s < len(steps):
@@ -231,7 +233,7 @@
     shards = lax.axis_size("fsdp")
     group = shards // replicas
     piece = momentum.shape[1]
-    per = next(n for n in (4, 2, 1) if piece % (n * LANES) == 0)
+    per = next(n for n in (7, 1) if piece % (n * LANES) == 0)
     chunks = group * per
     quarter = cols // replicas
     dma = pltpu.SemaphoreType.DMA

time: 81.6 us -> 70.3 us (0.86)
  Pallas kernels: 74.8 us -> 63.6 us
    pallas_call x1, Pallas kernels: 74.8 us -> 63.6 us  [per_device(): pl.pallas_call(functools.partial(sync_kernel, replicas, shards, per), out...]
where the time goes in v4:
time: 70.3 us; the launch traced here: 70.2 us
  Pallas kernels  63.6 us (90%)
  other arithmetic  3.23 us (5%)
  local copies, waits for them, and re-layouts  2.67 us (4%)
    pallas_call x1, Pallas kernels, per_device(): pl.pallas_call(functools.partial(sync_kernel, replicas, shards, per), out...  63.6 us
    unnamed x6, local copies, waits for them, and re-layouts  2.67 us
    sub x1, other arithmetic, per_device(): new_weights = base_weights - gathered.astype(jnp.float32)  2.14 us

profile of v4, /device:TPU:7, one launch (start us, length us, event | category | flops | bytes accessed | tf_op | source)
XLA Modules:
  0.0 70.2 jit_solution(16550268969642269011)
XLA Ops:
  0.6 0.0 copy-start
  0.6 1.2 %copy-done = f32[64,3584]{1,0:T(8,128)S(1)} copy-done((f32[64,3584]{1,0:T(8,128)S(1)}, f32[64,3584]{1,0:T(8,128)}, u32[]{:S(2)}) %copy-start) | copy-done | bytes 917528
  1.8 0.0 copy-start.1
  1.8 1.5 %copy-done.1 = bf16[1,32,28672]{2,1,0:T(8,128)(2,1)S(1)} copy-done((bf16[1,32,28672]{2,1,0:T(8,128)(2,1)S(1)}, bf16[1,32,28672]{2,1,0:T(8,128)(2,1)}, u32[]{:S(2)}) %copy-start.1) | copy-done | bytes 1835032
  3.3 0.0 copy-start.2
  3.3 63.6 %shard_map.50 = (bf16[32,28672]{1,0:T(8,128)(2,1)S(1)}, bf16[64,3584]{1,0:T(8,128)(2,1)S(1)}) custom-call(bf16[32,28672]{1,0:T(8,128)(2,1)S(1)} %bitcast.1, f32[32,28672]{1,0:T(8,128)} %base.1, f32[64,3584]{1,0:T(8,128)S(1)} %copy-done), custom_call_target="tpu_custom_call" | custom-call | tf_op jit(solution)/shard_map/pallas_call | solution.py:240
  66.9 0.0 copy-done.2
  66.9 2.1 %convert_subtract_fusion = f32[32,28672]{1,0:T(8,128)} fusion(f32[32,28672]{1,0:T(8,128)S(1)} %copy-done.2, bf16[32,28672]{1,0:T(8,128)(2,1)S(1)} %get-tuple-element.4), kind=kLoop, calls=%fused_computation | loop fusion | flops 1835008 | bytes 9175040 | tf_op jit(solution)/shard_map/sub | solution.py:267
  69.1 1.1 %add_multiply_fusion = f32[64,3584]{1,0:T(8,128)} fusion(bf16[64,3584]{1,0:T(8,128)(2,1)S(1)} %get-tuple-element.5, f32[64,3584]{1,0:T(8,128)S(1)} %copy-done), kind=kLoop, calls=%fused_computation.1 | loop fusion | flops 1146880 | bytes 2293760 | tf_op jit(solution)/shard_map/div | solution.py:268
Async XLA Ops:
  0.6 1.2 %copy-start = (f32[64,3584]{1,0:T(8,128)S(1)}, f32[64,3584]{1,0:T(8,128)}, u32[]{:S(2)}) copy-start(f32[64,3584]{1,0:T(8,128)} %mom_full.1) | copy-start | bytes 2752516
  1.8 1.5 %copy-start.1 = (bf16[1,32,28672]{2,1,0:T(8,128)(2,1)S(1)}, bf16[1,32,28672]{2,1,0:T(8,128)(2,1)}, u32[]{:S(2)}) copy-start(bf16[1,32,28672]{2,1,0:T(8,128)(2,1)} %param.3) | copy-start | bytes 5505028
  3.3 63.6 %copy-start.2 = (f32[32,28672]{1,0:T(8,128)S(1)}, f32[32,28672]{1,0:T(8,128)}, u32[]{:S(2)}) copy-start(f32[32,28672]{1,0:T(8,128)} %base.1) | copy-start | bytes 11010052
